TPU v7x, 32 devices: a whole 2x2x4 slice. The times are simulated.
32 devices in a mesh: dp: 8 (over y, x, core), tensor: 4 (over z).
Axes of the slice: x: 2, y: 2, z: 4, core: 2. Of those that a mesh axis runs over, the one named last changes fastest.
Arguments:
- tokens: bfloat16 [3072, 8192], P('dp', 'tensor'), may hold values from -6 to 6
- w_kv: bfloat16 [8192, 2048], P('tensor'), may hold values from -0.0625 to 0.0625
- a_store: bfloat16 [256, 16, 8192], P('dp', None, 'tensor'), may hold values from -0.0625 to 0.0625
- b_store: bfloat16 [256, 16, 2048], P('dp', None, 'tensor'), may hold values from -1.5 to 1.5
- row_peer: int32 [3072, 1], P('dp'), may hold values from 0 to 7; in each aligned block of 384 rows (0 to 383, 384 to 767, ...) at most 96 rows name the same one
- wanted: int32 [8, 8], replicated, may hold values from 0 to 31
- live_rows: int32 [8], P('dp'), may hold values from 1 to 384, 1536 in all
Outputs:
- kv_out: float32 [3072, 2048], P('dp', 'tensor')
Inputs may be any that keep to these rules, and one draw needn't show every extreme that they name: `row_peer`: within one group of 384 rows no owner is named by more than 96 rows, a bound that some block reaches.
All inputs are finite; a program needn't handle non-finite values. No bound on the sum of `live_rows` on one device may be relied on, other than what follows from the above.
Results may differ from a plain program's by a relative error of at most 0.0003.
Values may be sent and summed in bfloat16 or wider, within the bound.
A program may use at most 64 MiB of HBM per device.

v0:
```python
import functools
import jax
import jax.numpy as jnp
from jax import lax
from jax.experimental import pallas as pl
from jax.experimental.pallas import tpu as pltpu
from jax.sharding import PartitionSpec as P

MESH = pl.DeviceIdType.MESH
LINK = jnp.int16
STEPS = 32766.0
LEAST = 1e-30
CHUNKS = 2
LAG = 1


def encode(x):
    top = jnp.maximum(jnp.max(jnp.abs(x), axis=0, keepdims=True), LEAST)
    code = jnp.round(x * (STEPS / top)).astype(jnp.int32).astype(LINK)
    return code, top * (1.0 / STEPS)


def decode(code, step):
    return code.astype(jnp.int32).astype(jnp.float32) * step


def kernel(n, owners, wanted, tok_hbm, w_hbm, a_hbm, b_hbm, peer_ref, out_ref,
           tok, w, a_vm, b_vm, part, zs, zr, us, ur, a_out, a_in, b_out, b_in, s_out, s_in,
           tok_sem, w_sem, a_sem, b_sem, zs_sem, zr_sem, us_sem, ur_sem, as_sem, ar_sem, bs_sem, br_sem,
           ss_sem, sr_sem):
    p = lax.axis_index("tensor")
    me = lax.axis_index("dp")
    rows = tok.shape[0]
    blk = w.shape[2]
    rank = a_vm.shape[1]
    ch = zs.shape[2]
    rc = rows // ch

    def w_copy(d):
        cols = pl.ds(pl.multiple_of(d * blk, blk), blk)
        return pltpu.make_async_copy(w_hbm.at[:, cols], w.at[d], w_sem.at[d])

    def place(t):
        s = t // 2
        way = t % 2
        d = jnp.where(way == 0, n - 1 - s, s)
        return s, way, d

    def ahead(way, d):
        return ((way == 0) & (d > p)) | ((way == 1) & (d < p))

    def first_hop(way):
        return ((way == 0) & (p == 0)) | ((way == 1) & (p == n - 1))

    def z_copy(way, s, c, q):
        return pltpu.make_async_remote_copy(
            src_ref=zs.at[way, s, c], dst_ref=zr.at[way, s, c],
            send_sem=zs_sem.at[way, s, c], recv_sem=zr_sem.at[way, s, c],
            device_id={"tensor": q}, device_id_type=MESH)

    def u_copy(way, s, c, q):
        return pltpu.make_async_remote_copy(
            src_ref=us.at[way, s, c], dst_ref=ur.at[way, s, c],
            send_sem=us_sem.at[way, s, c], recv_sem=ur_sem.at[way, s, c],
            device_id={"tensor": q}, device_id_type=MESH)

    def put(way, s, c, q, value):
        code, step = encode(value)
        us[way, s, c] = step
        zs[way, s, c] = code
        u_copy(way, s, c, q).start()
        z_copy(way, s, c, q).start()

    def get(way, s, c, q):
        u_copy(way, s, c, q).wait_recv()
        z_copy(way, s, c, q).wait_recv()
        return decode(zr[way, s, c], ur[way, s, c])

    def a_copy(j, slot):
        return pltpu.make_async_remote_copy(
            src_ref=a_out.at[j], dst_ref=a_in.at[slot],
            send_sem=as_sem.at[j], recv_sem=ar_sem.at[slot],
            device_id={"dp": j}, device_id_type=MESH)

    def b_copy(j, slot):
        return pltpu.make_async_remote_copy(
            src_ref=b_out.at[j], dst_ref=b_in.at[slot],
            send_sem=bs_sem.at[j], recv_sem=br_sem.at[slot],
            device_id={"dp": j}, device_id_type=MESH)

    def s_copy(q, slot):
        return pltpu.make_async_remote_copy(
            src_ref=s_out, dst_ref=s_in.at[slot],
            send_sem=ss_sem.at[q], recv_sem=sr_sem.at[slot],
            device_id={"tensor": q}, device_id_type=MESH)

    barrier = pltpu.get_barrier_semaphore()

    @pl.loop(1, owners)
    def _(k):
        pl.semaphore_signal(barrier, inc=1, device_id={"dp": lax.rem(me + k, owners)},
                            device_id_type=MESH)

    @pl.loop(1, n)
    def _(k):
        pl.semaphore_signal(barrier, inc=1, device_id={"tensor": lax.rem(p + k, n)},
                            device_id_type=MESH)

    tok_copy = pltpu.make_async_copy(tok_hbm, tok, tok_sem)
    tok_copy.start()

    def load(t):
        s, way, d = place(t)

        @pl.when(ahead(way, d))
        def _():
            w_copy(d).start()

    pl.loop(0, 2)(load)
    a_load = pltpu.make_async_copy(a_hbm, a_vm, a_sem)
    b_load = pltpu.make_async_copy(b_hbm, b_vm, b_sem)
    tok_copy.wait()

    def multiply(d, c):
        span = pl.ds(pl.multiple_of(c * rc, rc), rc)
        part[d, span] = jnp.dot(tok[span], w[d], preferred_element_type=jnp.float32)

    @pl.loop(0, 2)
    def _(t):
        s, way, d = place(t)

        @pl.when(ahead(way, d))
        def _():
            w_copy(d).wait()

    a_load.start()
    b_load.start()
    pl.loop(2, 2 * (n - 1))(load)
    w_copy(p).start()

    @pl.loop(0, 2)
    def _(t):
        s, way, d = place(t)

        @pl.when(ahead(way, d))
        def _():
            multiply(d, 0)

    pl.semaphore_wait(barrier, owners - 1 + n - 1)

    def fetch():
        a_load.wait()
        b_load.wait()

        @pl.loop(0, owners)
        def _(k):
            j = lax.rem(me + k, owners)
            asked = wanted[j, me]
            a_map = a_vm[asked]
            b_map = b_vm[asked]

            @pl.when(k == 0)
            def _():
                a_in[me] = a_map
                b_in[me] = b_map

            @pl.when(k > 0)
            def _():
                a_out[j] = a_map
                b_out[j] = b_map
                a_copy(j, me).start()
                b_copy(j, me).start()

    def send_first(way, s, d, c):
        q = jnp.where(way == 0, p + 1, p - 1)
        put(way, s, c, q, part[d, pl.ds(pl.multiple_of(c * rc, rc), rc)])

    @pl.loop(0, 2 * (n - 1))
    def _(t):
        s, way, d = place(t)

        @pl.when(ahead(way, d))
        def _():
            @pl.when(t > 1)
            def _():
                w_copy(d).wait()

            @pl.loop(0, ch)
            def _(c):
                @pl.when((t > 1) | (c > 0))
                def _():
                    multiply(d, c)

                @pl.when(first_hop(way) & (s < n - 2))
                def _():
                    send_first(way, s, d, c)

        @pl.when(t == 1)
        def _():
            fetch()

    w_copy(p).wait()
    out_ref[...] = jnp.dot(tok[...], w[p], preferred_element_type=jnp.float32)

    def pass_on(s, c, way):
        d = jnp.where(way == 0, n - 1 - s, s)
        span = pl.ds(pl.multiple_of(c * rc, rc), rc)
        q = jnp.where(way == 0, p + 1, p - 1)
        back = jnp.where(way == 0, p - 1, p + 1)

        @pl.when(jnp.logical_not(first_hop(way)) & ahead(way, d))
        def _():
            put(way, s, c, q, get(way, s, c, back) + part[d, span])

        @pl.when(jnp.logical_not(first_hop(way)) & (d == p))
        def _():
            out_ref[span] += get(way, s, c, back)

    near = jnp.where(2 * p < n - 1, 0, 1)
    lag = LAG * jnp.abs(n - 1 - 2 * p)
    late = LAG * (n - 1)

    def pass_range(low, high):
        @pl.loop(low, high)
        def _(i):
            @pl.when(i < (n - 1) * ch)
            def _():
                pass_on(i // ch, i % ch, near)

            k = i - lag

            @pl.when((k >= 0) & (k < (n - 1) * ch))
            def _():
                pass_on(k // ch, k % ch, 1 - near)

    pass_range(0, ch)

    @pl.loop(1, owners)
    def _(k):
        a_copy(lax.rem(me + k, owners), lax.rem(me + k, owners)).wait()

    width = owners * rank
    named = peer_ref[...]
    mine = lax.broadcasted_iota(jnp.int32, (width, rows), 0) // rank == named
    every = lax.dot_general(a_in[...].reshape(width, a_in.shape[2]), tok[...],
                            (((1,), (1,)), ((), ())), preferred_element_type=jnp.float32)
    kept = jnp.where(mine, every, 0.0).reshape(owners, rank, rows)
    total = kept[0]
    for j in range(1, owners):
        total = total + kept[j]
    s_out[...] = total

    @pl.loop(1, n)
    def _(k):
        q = lax.rem(p + k, n)
        s_copy(q, p).start()

    for way in range(2):
        s = n - 2
        d = n - 1 - s if way == 0 else s

        @pl.when(first_hop(way))
        def _():
            for c in range(ch):
                send_first(way, s, d, c)

    pass_range(ch, (n - 2) * ch)

    @pl.loop(1, owners)
    def _(k):
        b_copy(lax.rem(me + k, owners), lax.rem(me + k, owners)).wait()

    @pl.loop(1, n)
    def _(k):
        q = lax.rem(p + k, n)
        s_copy(q, q).wait()
    total = s_out[...]
    for k in range(1, n):
        total = total + s_in[lax.rem(p + k, n)]
    spread = jnp.broadcast_to(total[None], (owners, rank, rows)).reshape(width, rows)
    shrink = jnp.where(mine, spread, 0.0).T
    high = shrink.astype(jnp.bfloat16)
    low = (shrink - high.astype(jnp.float32)).astype(jnp.bfloat16)
    ups = b_in[...].reshape(width, blk)
    out_ref[...] += (jnp.dot(high, ups, preferred_element_type=jnp.float32)
                     + jnp.dot(low, ups, preferred_element_type=jnp.float32))

    pass_range((n - 2) * ch, (n - 1) * ch + late)

    @pl.loop(0, 2 * (n - 1))
    def _(t):
        s, way, d = place(t)

        @pl.when(ahead(way, d))
        def _():
            for c in range(ch):
                q = jnp.where(way == 0, p + 1, p - 1)
                u_copy(way, s, c, q).wait_send()
                z_copy(way, s, c, q).wait_send()


def local(n, owners, tokens, w_kv, a_store, b_store, row_peer, wanted, live_rows):
    rows, feat = tokens.shape
    blk = w_kv.shape[1] // n
    held, rank = a_store.shape[:2]
    rc = rows // CHUNKS
    vmem, dma = pltpu.VMEM, pltpu.SemaphoreType.DMA
    anyspec = pl.BlockSpec(memory_space=pl.ANY)
    out = pl.pallas_call(
        functools.partial(kernel, n, owners),
        out_shape=jax.ShapeDtypeStruct((rows, blk), jnp.float32),
        in_specs=[pl.BlockSpec(memory_space=pltpu.SMEM), anyspec, anyspec, anyspec, anyspec,
                  pl.BlockSpec(memory_space=pltpu.VMEM)],
        out_specs=pl.BlockSpec(memory_space=pltpu.VMEM),
        scratch_shapes=[
            vmem((rows, feat), jnp.bfloat16),
            vmem((n, feat, blk), jnp.bfloat16),
            vmem((held, rank, feat), jnp.bfloat16),
            vmem((held, rank, blk), jnp.bfloat16),
            vmem((n, rows, blk), jnp.float32),
            vmem((2, n - 1, CHUNKS, rc, blk), LINK),
            vmem((2, n - 1, CHUNKS, rc, blk), LINK),
            vmem((2, n - 1, CHUNKS, 1, blk), jnp.float32),
            vmem((2, n - 1, CHUNKS, 1, blk), jnp.float32),
            vmem((owners, rank, feat), jnp.bfloat16),
            vmem((owners, rank, feat), jnp.bfloat16),
            vmem((owners, rank, blk), jnp.bfloat16),
            vmem((owners, rank, blk), jnp.bfloat16),
            vmem((rank, rows), jnp.float32),
            vmem((n, rank, rows), jnp.float32),
            dma, dma((n,)), dma, dma,
            dma((2, n - 1, CHUNKS)), dma((2, n - 1, CHUNKS)),
            dma((2, n - 1, CHUNKS)), dma((2, n - 1, CHUNKS)),
            dma((owners,)), dma((owners,)), dma((owners,)), dma((owners,)),
            dma((n,)), dma((n,)),
        ],
        compiler_params=pltpu.CompilerParams(collective_id=0, has_side_effects=True),
        name="project",
    )(wanted, tokens, w_kv, a_store, b_store, row_peer.reshape(1, rows))
    inside = jnp.arange(rows, dtype=jnp.int32) < live_rows[0]
    return jnp.where(inside[:, None], out, 0.0)


def solution(mesh):
    in_specs = (
        P("dp", "tensor"),
        P("tensor", None),
        P("dp", None, "tensor"),
        P("dp", None, "tensor"),
        P("dp", None),
        P(),
        P("dp"),
    )
    body = functools.partial(local, mesh.shape["tensor"], mesh.shape["dp"])
    return jax.shard_map(body, mesh=mesh, in_specs=in_specs, out_specs=P("dp", "tensor"),
                         check_vma=False)
```

profile of v0, /device:TPU:0, one launch (start us, length us, event | category | flops | bytes accessed | tf_op | source)
XLA Modules:
  0.0 37.6 jit_solution(11933377343763980067)
XLA Ops:
  0.7 34.8 %project.1 = f32[384,512]{1,0:T(8,128)} custom-call(s32[8,8]{1,0:T(8,128)} %wanted.1, bf16[384,2048]{1,0:T(8,128)(2,1)} %tok_hbm.1, bf16[2048,2048]{1,0:T(8,128)(2,1)} %w_hbm.1, bf16[32,16,2048]{2,1,0:T(8,128)(2,1)} %a_hbm.1, bf16[32,16,512]{2,1,0:T(8,128)(2,1)} %b_hbm.1, s32[1,384]{1,0:T(1,128)} %bitcast.3), custom_call_target="tpu_custom_call" | custom-call | tf_op jit(solution)/shard_map/project/pallas_call | solution.py:309
  35.5 2.1 %broadcast_select_fusion = f32[384,512]{1,0:T(8,128)} fusion(f32[384,512]{1,0:T(8,128)} %project.1, pred[384]{0:T(512)(128)(4,1)S(1)} %iota_compare_fusion), kind=kLoop, calls=%fused_computation | loop fusion | flops 196608 | bytes 1573248 | tf_op jit(solution)/shard_map/jit(_where)/select_n | solution.py:341
  (1 shorter events, 0.0 us)
where the time goes:
time: 38.1 us; the launch traced here: 37.6 us
  Pallas kernels  34.8 us (91%)
  other arithmetic  2.14 us (6%)
  between operations  0.67 us (2%)
    pallas_call x1, Pallas kernels, local(): pl.pallas_call(functools.partial(kernel, n, owners), out_shape=jax.ShapeD...  34.8 us
    select_n x1, other arithmetic, local(): return jnp.where(inside[:, None], out, 0.0)  2.14 us

commit v1 on v0

--- a/solution.py
+++ b/solution.py
@@ -24,7 +24,7 @@
     return code.astype(jnp.int32).astype(jnp.float32) * step
 
 
-def kernel(n, owners, wanted, tok_hbm, w_hbm, a_hbm, b_hbm, peer_ref, out_ref,
+def kernel(n, owners, wanted, live, tok_hbm, w_hbm, a_hbm, b_hbm, peer_ref, out_ref,
            tok, w, a_vm, b_vm, part, zs, zr, us, ur, a_out, a_in, b_out, b_in, s_out, s_in,
            tok_sem, w_sem, a_sem, b_sem, zs_sem, zr_sem, us_sem, ur_sem, as_sem, ar_sem, bs_sem, br_sem,
            ss_sem, sr_sem):
@@ -286,6 +286,8 @@
                      + jnp.dot(low, ups, preferred_element_type=jnp.float32))
 
     pass_range((n - 2) * ch, (n - 1) * ch + late)
+    inside = lax.broadcasted_iota(jnp.int32, (rows, blk), 0) < live[0]
+    out_ref[...] = jnp.where(inside, out_ref[...], 0.0)
 
     @pl.loop(0, 2 * (n - 1))
     def _(t):
@@ -306,10 +308,10 @@
     rc = rows // CHUNKS
     vmem, dma = pltpu.VMEM, pltpu.SemaphoreType.DMA
     anyspec = pl.BlockSpec(memory_space=pl.ANY)
-    out = pl.pallas_call(
+    return pl.pallas_call(
         functools.partial(kernel, n, owners),
         out_shape=jax.ShapeDtypeStruct((rows, blk), jnp.float32),
-        in_specs=[pl.BlockSpec(memory_space=pltpu.SMEM), anyspec, anyspec, anyspec, anyspec,
+        in_specs=[pl.BlockSpec(memory_space=pltpu.SMEM), pl.BlockSpec(memory_space=pltpu.SMEM), anyspec, anyspec, anyspec, anyspec,
                   pl.BlockSpec(memory_space=pltpu.VMEM)],
         out_specs=pl.BlockSpec(memory_space=pltpu.VMEM),
         scratch_shapes=[
@@ -336,9 +338,7 @@
         ],
         compiler_params=pltpu.CompilerParams(collective_id=0, has_side_effects=True),
         name="project",
-    )(wanted, tokens, w_kv, a_store, b_store, row_peer.reshape(1, rows))
-    inside = jnp.arange(rows, dtype=jnp.int32) < live_rows[0]
-    return jnp.where(inside[:, None], out, 0.0)
+    )(wanted, live_rows, tokens, w_kv, a_store, b_store, row_peer.reshape(1, rows))
 
 
 def solution(mesh):

time: 38.1 us -> 38.1 us (level)
  other arithmetic: 2.14 us -> 0 us
  local copies, waits for them, and re-layouts: 0 us -> 2.06 us
    select_n x1 -> x0, other arithmetic: 2.14 us -> none  [local(): return jnp.where(inside[:, None], out, 0.0)]
    unnamed x0 -> x1, local copies, waits for them, and re-layouts: none -> 2.06 us
where the time goes in v1:
time: 38.1 us; the launch traced here: 37.5 us
  Pallas kernels  34.8 us (91%)
  local copies, waits for them, and re-layouts  2.06 us (5%)
  between operations  0.66 us (2%)
    pallas_call x1, Pallas kernels, local(): pl.pallas_call(functools.partial(kernel, n, owners), out_shape=jax.ShapeD...  34.8 us
    unnamed x1, local copies, waits for them, and re-layouts  2.06 us

profile of v1, /device:TPU:0, one launch (start us, length us, event | category | flops | bytes accessed | tf_op | source)
XLA Modules:
  0.0 37.5 jit_solution(14552081898915027720)
XLA Ops:
  0.7 34.8 %project.1 = f32[384,512]{1,0:T(8,128)} custom-call(s32[8,8]{1,0:T(8,128)} %wanted.1, s32[1]{0:T(128)S(6)} %copy.9.live, bf16[384,2048]{1,0:T(8,128)(2,1)} %tok_hbm.1, bf16[2048,2048]{1,0:T(8,128)(2,1)} %w_hbm.1, bf16[32,16,2048]{2,1,0:T(8,128)(2,1)} %a_hbm.1, bf16[32,16,512]{2,1,0:T(8,128)(2,1)} %b_hbm.1, s32[1,384]{1,0:T(1,128)} %bitcast.1), custom_call_target="tpu_custom_call" | custom-call | tf_op jit(solution)/shard_map/project/pallas_call | solution.py:311
  35.5 2.1 %copy.10 = f32[384,512]{1,0:T(8,128)} copy(f32[384,512]{1,0:T(8,128)} %project.1) | data formatting | bytes 1572864

commit v2 on v1

v2 whole, which is shorter than its diff:
```python
import functools
import jax
import numpy as np
import jax.numpy as jnp
from jax import lax
from jax.experimental import pallas as pl
from jax.experimental.pallas import tpu as pltpu
from jax.sharding import PartitionSpec as P

MESH = pl.DeviceIdType.MESH
LINK = jnp.int16
STEPS = 32766.0
LEAST = 1e-30
LAG = 1
TILE = 8
SPLIT = 2


def most_pooled(owners, rows, home):
    total = owners * rows // 2
    lengths = np.arange(1, rows + 1)
    best = np.full(total + 1, -1)
    best[0] = 0
    for turn in range(owners):
        got = sum(np.clip(lengths - home - TILE * b, 0, TILE)
                  for b in range(turn, (rows - home) // TILE, owners))
        after = np.full(total + 1, -1)
        for length in range(1, rows + 1):
            before = best[:total + 1 - length]
            after[length:] = np.maximum(after[length:], np.where(before < 0, -1, before + got[length - 1]))
        best = after
    return int(best[total])


def plan(owners, rows):
    home = rows // 2
    cap = home // 2
    if home % (TILE * owners) == 0 and most_pooled(owners, rows, home) <= cap:
        return home, cap, cap // SPLIT
    return rows, 0, rows // 2


def encode(x):
    top = jnp.maximum(jnp.max(jnp.abs(x), axis=0, keepdims=True), LEAST)
    code = jnp.round(x * (STEPS / top)).astype(jnp.int32).astype(LINK)
    return code, top * (1.0 / STEPS)


def decode(code, step):
    return code.astype(jnp.int32).astype(jnp.float32) * step


def kernel(n, owners, home, cap, wanted, live, tok_hbm, w_hbm, a_hbm, b_hbm, peer_ref, out_ref,
           tok, w, a_vm, b_vm, part, zs, zr, us, ur, a_out, a_in, b_out, b_in, s_out, s_in,
           pin, picked, sel, spread_sel, n_out, n_in, r_out, r_in, v_out, v_in,
           tok_sem, w_sem, a_sem, b_sem, zs_sem, zr_sem, us_sem, ur_sem, as_sem, ar_sem, bs_sem, br_sem,
           ss_sem, sr_sem, ts_sem, tr_sem, own_sem, ns_sem, nr_sem, rs_sem, rr_sem, vs_sem, vr_sem):
    p = lax.axis_index("tensor")
    me = lax.axis_index("dp")
    rows = tok.shape[0]
    blk = w.shape[2]
    rank = a_vm.shape[1]
    ch = zs.shape[2]
    rc = zs.shape[3]
    hc = home // rc
    pc = cap // rc
    pool = rows - home
    per = pool // owners
    turns = per // TILE
    edge = (p == 0) | (p == n - 1)

    def w_copy(d):
        cols = pl.ds(pl.multiple_of(d * blk, blk), blk)
        return pltpu.make_async_copy(w_hbm.at[:, cols], w.at[d], w_sem.at[d])

    def place(t):
        s = t // 2
        way = t % 2
        d = jnp.where(way == 0, n - 1 - s, s)
        return s, way, d

    def ahead(way, d):
        return ((way == 0) & (d > p)) | ((way == 1) & (d < p))

    def first_hop(way):
        return ((way == 0) & (p == 0)) | ((way == 1) & (p == n - 1))

    def z_copy(way, s, c, q):
        return pltpu.make_async_remote_copy(
            src_ref=zs.at[way, s, c], dst_ref=zr.at[way, s, c],
            send_sem=zs_sem.at[way, s, c], recv_sem=zr_sem.at[way, s, c],
            device_id={"tensor": q}, device_id_type=MESH)

    def u_copy(way, s, c, q):
        return pltpu.make_async_remote_copy(
            src_ref=us.at[way, s, c], dst_ref=ur.at[way, s, c],
            send_sem=us_sem.at[way, s, c], recv_sem=ur_sem.at[way, s, c],
            device_id={"tensor": q}, device_id_type=MESH)

    def put(way, s, c, q, value):
        code, step = encode(value)
        us[way, s, c] = step
        zs[way, s, c] = code
        u_copy(way, s, c, q).start()
        z_copy(way, s, c, q).start()

    def get(way, s, c, q):
        u_copy(way, s, c, q).wait_recv()
        z_copy(way, s, c, q).wait_recv()
        return decode(zr[way, s, c], ur[way, s, c])

    def dp_copy(src, dst, send, recv, j):
        return pltpu.make_async_remote_copy(
            src_ref=src, dst_ref=dst, send_sem=send, recv_sem=recv,
            device_id={"dp": j}, device_id_type=MESH)

    def a_copy(j, slot):
        return dp_copy(a_out.at[j], a_in.at[slot], as_sem.at[j], ar_sem.at[slot], j)

    def b_copy(j, slot):
        return dp_copy(b_out.at[j], b_in.at[slot], bs_sem.at[j], br_sem.at[slot], j)

    def n_copy(j, slot):
        return dp_copy(n_out, n_in.at[slot], ns_sem.at[j], nr_sem.at[slot], j)

    def r_copy(j, slot):
        return dp_copy(r_out.at[j], r_in.at[slot], rs_sem.at[j], rr_sem.at[slot], j)

    def v_copy(j, slot):
        return dp_copy(v_out, v_in.at[slot], vs_sem.at[j], vr_sem.at[slot], j)

    def source_rows(j, turn):
        b = lax.rem(j - me + owners, owners) + owners * turn
        return tok_hbm.at[pl.ds(pl.multiple_of(home + TILE * b, TILE), TILE), :]

    def slot_rows(slot, turn):
        return pin.at[pl.ds(pl.multiple_of(slot * per + TILE * turn, TILE), TILE), :]

    def t_copy(j, slot, turn):
        return dp_copy(source_rows(j, turn), slot_rows(slot, turn), ts_sem.at[j, turn], tr_sem.at[slot, turn], j)

    def own_copy(turn):
        return pltpu.make_async_copy(source_rows(me, turn), slot_rows(me, turn), own_sem.at[turn])

    def s_copy(q, slot):
        return pltpu.make_async_remote_copy(
            src_ref=s_out, dst_ref=s_in.at[slot],
            send_sem=ss_sem.at[q], recv_sem=sr_sem.at[slot],
            device_id={"tensor": q}, device_id_type=MESH)

    def others(body):
        @pl.loop(1, owners)
        def _(k):
            body(lax.rem(me + k, owners))

    barrier = pltpu.get_barrier_semaphore()

    @pl.loop(1, owners)
    def _(k):
        pl.semaphore_signal(barrier, inc=1, device_id={"dp": lax.rem(me + k, owners)},
                            device_id_type=MESH)

    @pl.loop(1, n)
    def _(k):
        pl.semaphore_signal(barrier, inc=1, device_id={"tensor": lax.rem(p + k, n)},
                            device_id_type=MESH)

    tok_copy = pltpu.make_async_copy(tok_hbm, tok, tok_sem)
    tok_copy.start()

    def load(t):
        s, way, d = place(t)

        @pl.when(ahead(way, d))
        def _():
            w_copy(d).start()

    pl.loop(0, 2 * (n - 1))(load)
    w_copy(p).start()
    a_load = pltpu.make_async_copy(a_hbm, a_vm, a_sem)
    b_load = pltpu.make_async_copy(b_hbm, b_vm, b_sem)
    a_load.start()
    b_load.start()

    if pool:
        n_out[...] = jnp.full(n_out.shape, live[0], jnp.int32)
        for turn in range(turns):
            own_copy(turn).start()

    pl.semaphore_wait(barrier, owners - 1 + n - 1)

    if pool:
        def scatter(j):
            n_copy(j, me).start()
            for turn in range(turns):
                t_copy(j, me, turn).start()

        others(scatter)
        n_in[me] = n_out[...]

    tok_copy.wait()

    def send_first(way, s, d, c):
        q = jnp.where(way == 0, p + 1, p - 1)
        put(way, s, c, q, part[d, pl.ds(pl.multiple_of(c * rc, rc), rc)])

    @pl.loop(0, 2 * (n - 1))
    def _(t):
        s, way, d = place(t)

        @pl.when(ahead(way, d))
        def _():
            w_copy(d).wait()

            @pl.loop(0, SPLIT)
            def _(h):
                span = pl.ds(pl.multiple_of(h * (home // SPLIT), home // SPLIT), home // SPLIT)
                part[d, span] = jnp.dot(tok[span], w[d], preferred_element_type=jnp.float32)

                @pl.when(first_hop(way) & (s < n - 2))
                def _():
                    @pl.loop(0, hc // SPLIT)
                    def _(c):
                        send_first(way, s, d, h * (hc // SPLIT) + c)

    a_load.wait()
    b_load.wait()

    @pl.loop(0, owners)
    def _(k):
        j = lax.rem(me + k, owners)
        asked = wanted[j, me]
        a_map = a_vm[asked]
        b_map = b_vm[asked]

        @pl.when(k == 0)
        def _():
            a_in[me] = a_map
            b_in[me] = b_map

        @pl.when(k > 0)
        def _():
            a_out[j] = a_map
            b_out[j] = b_map
            a_copy(j, me).start()
            b_copy(j, me).start()

    w_copy(p).wait()
    part[p, pl.ds(0, home)] = jnp.dot(tok[pl.ds(0, home)], w[p], preferred_element_type=jnp.float32)

    def pass_on(s, c, way):
        d = jnp.where(way == 0, n - 1 - s, s)
        span = pl.ds(pl.multiple_of(c * rc, rc), rc)
        q = jnp.where(way == 0, p + 1, p - 1)
        back = jnp.where(way == 0, p - 1, p + 1)

        @pl.when(jnp.logical_not(first_hop(way)) & ahead(way, d))
        def _():
            put(way, s, c, q, get(way, s, c, back) + part[d, span])

        @pl.when(jnp.logical_not(first_hop(way)) & (d == p))
        def _():
            part[p, span] += get(way, s, c, back)

    near = jnp.where(2 * p < n - 1, 0, 1)
    lag = LAG * jnp.abs(n - 1 - 2 * p)
    late = LAG * (n - 1)
    early = (n - 2) * hc
    mid = (n - 1) * pc
    count = (n - 1) * ch
    done = early + max(mid, pc + late)

    def item(i):
        if not pool:
            return lax.div(i, hc), lax.rem(i, hc)
        k = i - early
        m = k - mid
        s = jnp.where(k < 0, lax.div(i, hc), jnp.where(m < 0, lax.div(k, pc), n - 2))
        c = jnp.where(k < 0, lax.rem(i, hc), jnp.where(m < 0, hc + lax.rem(k, pc), m))
        return s, c

    def pass_range(low, high):
        @pl.loop(low, high)
        def _(i):
            @pl.when(i < count)
            def _():
                s, c = item(i)
                pass_on(s, c, near)

            k = i - lag

            @pl.when((k >= 0) & (k < count))
            def _():
                s, c = item(k)
                pass_on(s, c, 1 - near)

    pass_range(0, early)

    def last_home(low, high):
        for way in range(2):
            s = n - 2
            d = n - 1 - s if way == 0 else s

            @pl.when(first_hop(way))
            def _():
                @pl.loop(low, high)
                def _(c):
                    send_first(way, s, d, c)

    if pool:
        for turn in range(turns):
            own_copy(turn).wait()

        def collect(j):
            n_copy(j, j).wait()
            for turn in range(turns):
                t_copy(j, j, turn).wait()

        others(collect)

        def taken(shape, dim):
            slot = lax.broadcasted_iota(jnp.int32, shape, dim)
            owner = slot // per
            r = slot % per
            held = jnp.zeros(shape, jnp.int32)
            for i in range(owners):
                held = jnp.where(owner == i, n_in[i][0:1, 0:1], held)
            b = (me - owner + owners) % owners + owners * (r // TILE)
            return home + TILE * b + r % TILE < held

        first = lax.broadcasted_iota(jnp.int32, (pool, pool), 0)
        second = lax.broadcasted_iota(jnp.int32, (pool, pool), 1)

        def ones(mask):
            return jnp.where(mask, 1.0, 0.0).astype(jnp.bfloat16)

        valid = taken((cap, pool), 1)
        spot = jnp.dot(ones(valid), ones(first < second), preferred_element_type=jnp.float32).astype(jnp.int32)
        sel[...] = ones(valid & (spot == lax.broadcasted_iota(jnp.int32, (cap, pool), 0)))
        valid = taken((pool, cap), 0)
        spot = jnp.dot(ones(second < first), ones(valid), preferred_element_type=jnp.float32).astype(jnp.int32)
        spread_sel[...] = ones(valid & (spot == lax.broadcasted_iota(jnp.int32, (pool, cap), 1)))
        picked[...] = jnp.dot(sel[...], pin[...], preferred_element_type=jnp.float32).astype(jnp.bfloat16)

        @pl.loop(0, 2 * (n - 1))
        def _(t):
            s, way, d = place(t)

            @pl.when(ahead(way, d))
            def _():
                part[d, pl.ds(home, cap)] = jnp.dot(picked[...], w[d], preferred_element_type=jnp.float32)

                @pl.when(first_hop(way))
                def _():
                    @pl.loop(0, pc)
                    def _(c):
                        send_first(way, s, d, hc + c)

        part[p, pl.ds(home, cap)] = jnp.dot(picked[...], w[p], preferred_element_type=jnp.float32)

    last_home(0, hc // 2)
    split = jnp.where(edge, early, done)
    if pool:
        pass_range(early, split)

    others(lambda j: a_copy(j, j).wait())

    width = owners * rank
    named = peer_ref[...]
    mine = lax.broadcasted_iota(jnp.int32, (width, rows), 0) // rank == named
    every = lax.dot_general(a_in[...].reshape(width, a_in.shape[2]), tok[...],
                            (((1,), (1,)), ((), ())), preferred_element_type=jnp.float32)
    kept = jnp.where(mine, every, 0.0).reshape(owners, rank, rows)
    total = kept[0]
    for j in range(1, owners):
        total = total + kept[j]
    s_out[...] = total

    @pl.loop(1, n)
    def _(k):
        q = lax.rem(p + k, n)
        s_copy(q, p).start()

    last_home(hc // 2, hc)

    if pool:
        pass_range(split, done)
        full = part[p, pl.ds(home, cap)]
        top = jnp.maximum(jnp.max(jnp.abs(full), axis=0, keepdims=True), LEAST)
        code = jnp.round(full * (STEPS / top))
        upper = jnp.floor(code * (1.0 / 256.0))
        lower = code - 256.0 * upper
        wide = (256.0 * jnp.dot(spread_sel[...], upper.astype(jnp.bfloat16), preferred_element_type=jnp.float32)
                + jnp.dot(spread_sel[...], lower.astype(jnp.bfloat16), preferred_element_type=jnp.float32))
        v_out[...] = top * (1.0 / STEPS)
        r_out[...] = wide.reshape(owners, per, blk).astype(jnp.int32).astype(LINK)

        def give(j):
            v_copy(j, me).start()
            r_copy(j, me).start()

        others(give)
        v_in[me] = v_out[...]
        r_in[me] = r_out[me]

    others(lambda j: b_copy(j, j).wait())

    @pl.loop(1, n)
    def _(k):
        q = lax.rem(p + k, n)
        s_copy(q, q).wait()
    total = s_out[...]
    for k in range(1, n):
        total = total + s_in[lax.rem(p + k, n)]
    spread = jnp.broadcast_to(total[None], (owners, rank, rows)).reshape(width, rows)
    shrink = jnp.where(mine, spread, 0.0).T
    high = shrink.astype(jnp.bfloat16)
    low = (shrink - high.astype(jnp.float32)).astype(jnp.bfloat16)
    ups = b_in[...].reshape(width, blk)
    out_ref[...] = (jnp.dot(high, ups, preferred_element_type=jnp.float32)
                    + jnp.dot(low, ups, preferred_element_type=jnp.float32))

    pass_range(done if pool else early, count + late)

    def finish(low, size, value):
        span = pl.ds(low, size)
        inside = low + lax.broadcasted_iota(jnp.int32, (size, blk), 0) < live[0]
        out_ref[span] = jnp.where(inside, out_ref[span] + value, 0.0)

    finish(0, home, part[p, pl.ds(0, home)])
    if pool:
        def gather(j):
            v_copy(j, j).wait()
            r_copy(j, j).wait()

        others(gather)

        @pl.loop(0, owners)
        def _(k):
            j = lax.rem(me + k, owners)
            value = decode(r_in[j], v_in[j])
            for turn in range(turns):
                b = k + owners * turn
                finish(pl.multiple_of(home + TILE * b, TILE), TILE, value[turn * TILE:(turn + 1) * TILE])

    @pl.loop(0, 2 * (n - 1))
    def _(t):
        s, way, d = place(t)

        @pl.when(ahead(way, d))
        def _():
            @pl.loop(0, ch)
            def _(c):
                q = jnp.where(way == 0, p + 1, p - 1)
                u_copy(way, s, c, q).wait_send()
                z_copy(way, s, c, q).wait_send()


def local(n, owners, tokens, w_kv, a_store, b_store, row_peer, wanted, live_rows):
    rows, feat = tokens.shape
    blk = w_kv.shape[1] // n
    held, rank = a_store.shape[:2]
    home, cap, rc = plan(owners, rows)
    ch = (home + cap) // rc
    pool = max(rows - home, owners * TILE)
    spare = max(cap, TILE)
    per = pool // owners
    turns = per // TILE
    vmem, dma = pltpu.VMEM, pltpu.SemaphoreType.DMA
    anyspec = pl.BlockSpec(memory_space=pl.ANY)
    return pl.pallas_call(
        functools.partial(kernel, n, owners, home, cap),
        out_shape=jax.ShapeDtypeStruct((rows, blk), jnp.float32),
        in_specs=[pl.BlockSpec(memory_space=pltpu.SMEM), pl.BlockSpec(memory_space=pltpu.SMEM), anyspec, anyspec, anyspec, anyspec,
                  pl.BlockSpec(memory_space=pltpu.VMEM)],
        out_specs=pl.BlockSpec(memory_space=pltpu.VMEM),
        scratch_shapes=[
            vmem((rows, feat), jnp.bfloat16),
            vmem((n, feat, blk), jnp.bfloat16),
            vmem((held, rank, feat), jnp.bfloat16),
            vmem((held, rank, blk), jnp.bfloat16),
            vmem((n, home + cap, blk), jnp.float32),
            vmem((2, n - 1, ch, rc, blk), LINK),
            vmem((2, n - 1, ch, rc, blk), LINK),
            vmem((2, n - 1, ch, 1, blk), jnp.float32),
            vmem((2, n - 1, ch, 1, blk), jnp.float32),
            vmem((owners, rank, feat), jnp.bfloat16),
            vmem((owners, rank, feat), jnp.bfloat16),
            vmem((owners, rank, blk), jnp.bfloat16),
            vmem((owners, rank, blk), jnp.bfloat16),
            vmem((rank, rows), jnp.float32),
            vmem((n, rank, rows), jnp.float32),
            vmem((pool, feat), jnp.bfloat16),
            vmem((spare, feat), jnp.bfloat16),
            vmem((spare, pool), jnp.bfloat16),
            vmem((pool, spare), jnp.bfloat16),
            vmem((TILE, 128), jnp.int32),
            vmem((owners, TILE, 128), jnp.int32),
            vmem((owners, per, blk), LINK),
            vmem((owners, per, blk), LINK),
            vmem((1, blk), jnp.float32),
            vmem((owners, 1, blk), jnp.float32),
            dma, dma((n,)), dma, dma,
            dma((2, n - 1, ch)), dma((2, n - 1, ch)),
            dma((2, n - 1, ch)), dma((2, n - 1, ch)),
            dma((owners,)), dma((owners,)), dma((owners,)), dma((owners,)),
            dma((n,)), dma((n,)),
            dma((owners, turns)), dma((owners, turns)), dma((turns,)),
            dma((owners,)), dma((owners,)), dma((owners,)), dma((owners,)), dma((owners,)), dma((owners,)),
        ],
        compiler_params=pltpu.CompilerParams(collective_id=0, has_side_effects=True),
        name="project",
    )(wanted, live_rows, tokens, w_kv, a_store, b_store, row_peer.reshape(1, rows))


def solution(mesh):
    in_specs = (
        P("dp", "tensor"),
        P("tensor", None),
        P("dp", None, "tensor"),
        P("dp", None, "tensor"),
        P("dp", None),
        P(),
        P("dp"),
    )
    body = functools.partial(local, mesh.shape["tensor"], mesh.shape["dp"])
    return jax.shard_map(body, mesh=mesh, in_specs=in_specs, out_specs=P("dp", "tensor"),
                         check_vma=False)
```

time: 38.1 us -> 46.6 us (1.22)
  Pallas kernels: 34.8 us -> 43.6 us
    pallas_call x1, Pallas kernels: 34.8 us -> 43.6 us  [local(): pl.pallas_call(functools.partial(kernel, n, owners, home, cap), out_shape...]
where the time goes in v2:
time: 46.6 us; the launch traced here: 46.4 us
  Pallas kernels  43.6 us (94%)
  local copies, waits for them, and re-layouts  2.06 us (4%)
  between operations  0.66 us (1%)
    pallas_call x1, Pallas kernels, local(): pl.pallas_call(functools.partial(kernel, n, owners, home, cap), out_shape...  43.6 us
    unnamed x1, local copies, waits for them, and re-layouts  2.06 us

profile of v2, /device:TPU:0, one launch (start us, length us, event | category | flops | bytes accessed | tf_op | source)
XLA Modules:
  0.0 46.4 jit_solution(12268940475581722526)
XLA Ops:
  0.7 43.6 %project.1 = f32[384,512]{1,0:T(8,128)} custom-call(s32[8,8]{1,0:T(8,128)} %wanted.1, s32[1]{0:T(128)S(6)} %copy.9.live, bf16[384,2048]{1,0:T(8,128)(2,1)} %tok_hbm.1, bf16[2048,2048]{1,0:T(8,128)(2,1)} %w_hbm.1, bf16[32,16,2048]{2,1,0:T(8,128)(2,1)} %a_hbm.1, bf16[32,16,512]{2,1,0:T(8,128)(2,1)} %b_hbm.1, s32[1,384]{1,0:T(1,128)} %bitcast.1), custom_call_target="tpu_custom_call" | custom-call | tf_op jit(solution)/shard_map/project/pallas_call | solution.py:471
  44.3 2.1 %copy.10 = f32[384,512]{1,0:T(8,128)} copy(f32[384,512]{1,0:T(8,128)} %project.1) | data formatting | bytes 1572864
